TPU v7x, 512 devices: a whole 4x8x8 slice. The times are simulated.
512 devices in a mesh: seq: 32 (over y, x), trow: 2 (over core), tcol: 8 (over z).
Axes of the slice: x: 4, y: 8, z: 8, core: 2. Of those that a mesh axis runs over, the one named last changes fastest.
Arguments:
- tokens: bfloat16 [16384, 4096], P('seq', ('trow', 'tcol')), may hold values from -24 to 24
- norm_gain: float32 [4096], replicated, may hold values from 0.1 to 1.9
- in_weight: bfloat16 [3, 4096, 8192], P(None, None, ('trow', 'tcol')), may hold values from -0.09375 to 0.09375
- filter_taps: float32 [128, 8192], P(None, ('trow', 'tcol')), may hold values from -0.5 to 0.5
- conv_skip: float32 [8192], P(('trow', 'tcol')), may hold values from -1 to 1
- out_weight: bfloat16 [8192, 4096], P(('trow', 'tcol')), may hold values from -0.09375 to 0.09375
Outputs:
- mixer_out: bfloat16 [16384, 4096], P('seq', ('trow', 'tcol'))
All inputs are finite; a program needn't handle non-finite values.
Results may differ from a plain program's by a relative error of at most 0.03.
Values may be sent and summed in bfloat16 or wider, within the bound.
A program may use at most 64 MiB of HBM per device.

v0:
```python
import jax
import jax.numpy as jnp
from jax import lax
from jax.sharding import PartitionSpec as P


def passed_along(block, axis, distance):
    devices = range(lax.axis_size(axis))
    route = [(i - distance, i) for i in devices if i - distance in devices]
    return lax.ppermute(block, axis, route)


def on_device(tokens, norm_gain, in_weight, filter_taps, conv_skip, out_weight):
    whole = lax.all_gather(tokens, ("trow", "tcol"), axis=1, tiled=True)
    wide = whole.astype(jnp.float32)
    mean_square = jnp.mean(wide * wide, axis=1, keepdims=True)
    normed = (wide * lax.rsqrt(mean_square + 1e-06) * norm_gain).astype(jnp.bfloat16)
    query = jnp.dot(normed, in_weight[0], preferred_element_type=jnp.float32).astype(jnp.bfloat16)
    keys = jnp.dot(normed, in_weight[1], preferred_element_type=jnp.float32).astype(jnp.bfloat16)
    values = jnp.dot(normed, in_weight[2], preferred_element_type=jnp.float32).astype(jnp.bfloat16)
    mixed = (keys.astype(jnp.float32) * values.astype(jnp.float32)).astype(jnp.bfloat16)
    taps = filter_taps.shape[0]
    rows = mixed.shape[0]
    channels = mixed.shape[1]
    tail_rows = mixed[rows - (taps - 1) :]
    previous = passed_along(tail_rows, "seq", 1)
    extended = jnp.concatenate([previous, mixed], axis=0)

    def tap_group(group, total):
        for inner in range(8):
            index = group * 8 + inner
            window = lax.dynamic_slice_in_dim(extended, taps - 1 - index, rows, 0)
            weight = lax.dynamic_slice_in_dim(filter_taps, index, 1, 0)
            total = total + window.astype(jnp.float32) * weight
        return total

    filtered = lax.fori_loop(0, taps // 8, tap_group, jnp.zeros((rows, channels), jnp.float32))
    filtered = filtered + conv_skip * mixed.astype(jnp.float32)
    gated = (query.astype(jnp.float32) * filtered).astype(jnp.bfloat16)
    partial_sum = jnp.dot(gated, out_weight, preferred_element_type=jnp.float32)
    summed = lax.psum_scatter(
        partial_sum.astype(jnp.bfloat16), ("trow", "tcol"), scatter_dimension=1, tiled=True
    )
    return summed


def solution(mesh):
    placed = (
        P("seq", ("trow", "tcol")),
        P(),
        P(None, None, ("trow", "tcol")),
        P(None, ("trow", "tcol")),
        P(("trow", "tcol")),
        P(("trow", "tcol"), None),
    )
    return jax.shard_map(
        on_device, mesh=mesh, in_specs=placed, out_specs=P("seq", ("trow", "tcol")), check_vma=False
    )
```

profile of v0, /device:TPU:1, one launch (start us, length us, event | category | flops | bytes accessed | tf_op | source)
XLA Modules:
  0.0 220.7 jit_solution(7478278523960679927)
XLA Ops:
  7.3 59.9 %all-gather.2.cloned.1.call-done = bf16[512,4096]{1,0:T(8,128)(2,1)} async-done(((bf16[512,256]{1,0:T(8,128)(2,1)}), bf16[512,4096]{1,0:T(8,128)(2,1)}) %all-gather.2.cloned.1.call-update) | async-done | bytes 4194320 | tf_op jit(solution)/shard_map/all_gather | solution.py:14
  67.2 3.2 %fusion.7 = f32[512]{0:T(512)S(1)} fusion(bf16[512,4096]{1,0:T(8,128)(2,1)} %all-gather.2.cloned.1.call-done), kind=kLoop, calls=%fused_computation.18 | loop fusion | flops 6290944 | bytes 4196352 | tf_op jit(solution)/shard_map/reduce_sum | solution.py:16
  70.6 4.6 %fusion.46 = f32[512,512]{1,0:T(8,128)S(1)} fusion(bf16[3,4096,512]{2,1,0:T(8,128)(2,1)} %param.10, bf16[512,4096]{1,0:T(8,128)(2,1)S(1)} %copy-done, f32[4096]{0:T(1024)S(1)} %copy-done.1, f32[512]{0:T(512)S(1)} %add_rsqrt_fusion), kind=kOutput, calls=%fused_computation.40 | convolution fusion | flops 2156396544 | bytes 9455616 | tf_op jit(solution)/shard_map/dot_general | solution.py:20
  75.2 4.6 %fusion.40 = bf16[512,512]{1,0:T(8,128)(2,1)S(1)} fusion(f32[512,512]{1,0:T(8,128)S(1)} %fusion.46, bf16[3,4096,512]{2,1,0:T(8,128)(2,1)} %param.10, bf16[512,4096]{1,0:T(8,128)(2,1)S(1)} %copy-done, f32[4096]{0:T(1024)S(1)} %copy-done.1, f32[512]{0:T(512)S(1)} %add_rsqrt_fusion), kind=kOutput, calls=%fused_computation.38 | convolution fusion | flops 2156920832 | bytes 9979904 | tf_op jit(solution)/shard_map/dot_general | solution.py:19
  79.8 3.1 %collective-permute-start = (bf16[127,512]{1,0:T(8,128)(2,1)S(1)}, bf16[127,512]{1,0:T(8,128)(2,1)S(1)}, u32[]{:S(2)}, u32[]{:S(2)}) collective-permute-start(bf16[127,512]{1,0:T(8,128)(2,1)S(1)} %slice.16), channel_id=1, source_target_pairs={{0,16},{16,32},{32,48},{48,64},{64,80},{80,96},{96,112},{112,128},... | collective-permute-start | bytes 390152 | tf_op jit(solution)/shard_map/ppermute | solution.py:10
  82.9 2.6 %collective-permute-done = bf16[127,512]{1,0:T(8,128)(2,1)S(1)} collective-permute-done((bf16[127,512]{1,0:T(8,128)(2,1)S(1)}, bf16[127,512]{1,0:T(8,128)(2,1)S(1)}, u32[]{:S(2)}, u32[]{:S(2)}) %collective-permute-start) | collective-permute-done | bytes 130080 | tf_op jit(solution)/shard_map/ppermute | solution.py:10
  85.6 39.9 %while.17 = (s32[]{:T(128)}, f32[512,512]{1,0:T(8,128)S(1)}, bf16[639,512]{1,0:T(8,128)(2,1)S(1)}, f32[128,512]{1,0:T(8,128)}, s32[]{:T(128)}, /*index=5*/s32[]{...) while((s32[]{:T(128)}, f32[512,512]{1,0:T(8,128)S(1)}, ...), condition=%wide.region_2.0_spmd.clone, body=%wide.region_1.0_spmd.clone.sunk | while | flops 6553667 | bytes 6341631 | solution.py:37
  85.7 1.0 constant_dynamic-slice_fusion.9
  86.8 1.4 fusion.58
  88.2 1.0 constant_dynamic-slice_fusion.9
  89.3 1.3 fusion.58
  91.8 1.4 fusion.58
  94.3 1.3 fusion.58
  95.7 1.0 constant_dynamic-slice_fusion.9
  96.8 1.4 fusion.58
  98.2 1.0 constant_dynamic-slice_fusion.9
  99.2 1.3 fusion.58
  101.7 1.4 fusion.58
  104.2 1.3 fusion.58
  105.7 1.0 constant_dynamic-slice_fusion.9
  106.7 1.4 fusion.58
  108.2 1.0 constant_dynamic-slice_fusion.9
  109.2 1.3 fusion.58
  111.7 1.4 fusion.58
  114.2 1.3 fusion.58
  115.7 1.0 constant_dynamic-slice_fusion.9
  116.7 1.4 fusion.58
  119.2 1.3 fusion.58
  121.7 1.4 fusion.58
  124.2 1.3 fusion.58
  125.5 11.2 %convolution_convert_fusion = bf16[512,4096]{1,0:T(8,128)(2,1)} fusion(bf16[512,4096]{1,0:T(8,128)(2,1)} %param.13, bf16[3,4096,512]{2,1,0:T(8,128)(2,1)} %param.10, f32[512,512]{1,0:T(8,128)S(1)} %get-tuple-element.156, bf16[512,512]{1,0:T(8,128)(2,1)S(1)} %fusion.40, f32[512]{0:T(512)S(1)} %copy-done.2, ...), kind=kOutput, calls=%fused_computation.21 | convolution fusion | flops 4307288064 | bytes 18370560 | tf_op jit(solution)/shard_map/dot_general | solution.py:40
  136.8 77.0 %reduce-scatter.2.cloned.1.call-done = bf16[512,256]{1,0:T(8,128)(2,1)} async-done(((bf16[512,4096]{1,0:T(8,128)(2,1)}), bf16[512,256]{1,0:T(8,128)(2,1)}) %reduce-scatter.2.cloned.1.call-update) | async-done | bytes 262160 | tf_op jit(solution)/shard_map/reduce_scatter | solution.py:41
  (23 shorter events, 10.5 us)
Async XLA Ops:
  6.5 63.9 %copy-start.1 = (f32[4096]{0:T(1024)S(1)}, f32[4096]{0:T(1024)}, u32[]{:S(2)}) copy-start(f32[4096]{0:T(1024)} %param.9) | copy-start | bytes 49156
  6.5 60.6 %all-gather.2.cloned.1.call-start = ((), (), s32[]{:S(2)}) async-start(), calls=%async_computation.1 | async-start | bytes 4456448 | tf_op jit(solution)/shard_map/all_gather | solution.py:14
  7.3 206.6 %reduce-scatter.2.cloned.1.call-start = ((), (), s32[]{:S(2)}) async-start(), calls=%async_computation.2 | async-start | bytes 4456448 | tf_op jit(solution)/shard_map/reduce_scatter | solution.py:41
  67.2 3.4 %copy-start = (bf16[512,4096]{1,0:T(8,128)(2,1)S(1)}, bf16[512,4096]{1,0:T(8,128)(2,1)}, u32[]{:S(2)}) copy-start(bf16[512,4096]{1,0:T(8,128)(2,1)} %all-gather.2.cloned.1.call-done) | copy-start | bytes 12582916
  79.8 5.7 %collective-permute-start = (bf16[127,512]{1,0:T(8,128)(2,1)S(1)}, bf16[127,512]{1,0:T(8,128)(2,1)S(1)}, u32[]{:S(2)}, u32[]{:S(2)}) collective-permute-start(bf16[127,512]{1,0:T(8,128)(2,1)S(1)} %slice.16), channel_id=1, source_target_pairs={{0,16},{16,32},{32,48},{48,64},{64,80},{80,96},{96,112},{112,128},... | collective-permute-start | bytes 390152 | tf_op jit(solution)/shard_map/ppermute | solution.py:10
  85.6 39.9 %copy-start.2 = (f32[512]{0:T(512)S(1)}, f32[512]{0:T(512)}, u32[]{:S(2)}) copy-start(f32[512]{0:T(512)} %param.12) | copy-start | bytes 6148
Sparse Core Ops, SparseCore 0:
  9.4 57.7 all-gather.1
  136.9 76.8 reduce-scatter.1
where the time goes:
time: 222 us; the launch traced here: 221 us
  waiting for transfers between devices  140 us (63%)
  other arithmetic  25 us (11%)
  matrix products  20.4 us (9%)
  local copies, waits for them, and re-layouts  16.9 us (8%)
  between operations  13.5 us (6%)
  starting transfers between devices  3.13 us (1%)
    reduce_scatter x1, waiting for transfers between devices, on_device(): lax.psum_scatter(partial_sum.astype(jnp.bfloat16), ('trow', 'tcol'), scat...  77 us
    all_gather x1, waiting for transfers between devices, on_device(): whole = lax.all_gather(tokens, ('trow', 'tcol'), axis=1, tiled=True)  59.9 us
    add x16, other arithmetic, tap_group(): total = total + window.astype(jnp.float32) * weight  21.6 us
    dynamic_slice x16, local copies, waits for them, and re-layouts, tap_group(): weight = lax.dynamic_slice_in_dim(filter_taps, index, 1, 0)  16.6 us
    dot_general x1, matrix products, on_device(): partial_sum = jnp.dot(gated, out_weight, preferred_element_type=jnp.float32)  11.2 us
    dot_general x1, matrix products, on_device(): jnp.dot(normed, in_weight[1], preferred_element_type=jnp.float32)  4.58 us
    dot_general x1, matrix products, on_device(): jnp.dot(normed, in_weight[2], preferred_element_type=jnp.float32)  4.56 us
  transfers between devices with their start and end apart: 3, of which 3 were waited for; matrix products, arithmetic and copies ran while one was open for 0% of the time, Pallas kernels for 0%

commit v1 on v0

--- a/solution.py
+++ b/solution.py
@@ -2,6 +2,27 @@
 import jax.numpy as jnp
 from jax import lax
 from jax.sharding import PartitionSpec as P
+
+
+def collect(x, axis, dim):
+    count, index, width = (lax.axis_size(axis), lax.axis_index(axis), x.shape[dim])
+    upward = [(i, (i + 1) % count) for i in range(count)]
+    backward = [(i, (i - 1) % count) for i in range(count)]
+    out = jnp.zeros((*x.shape[:dim], count * width, *x.shape[dim + 1 :]), x.dtype)
+    out = lax.dynamic_update_slice_in_dim(out, x, index * width, axis=dim)
+    from_left = from_right = x
+    halfway = count // 2
+    for hop in range(1, halfway + 1):
+        from_left = lax.ppermute(from_left, axis, upward)
+        out = lax.dynamic_update_slice_in_dim(
+            out, from_left, (index - hop) % count * width, axis=dim
+        )
+        if hop < count - halfway:
+            from_right = lax.ppermute(from_right, axis, backward)
+            out = lax.dynamic_update_slice_in_dim(
+                out, from_right, (index + hop) % count * width, axis=dim
+            )
+    return out
 
 
 def passed_along(block, axis, distance):
@@ -11,7 +32,7 @@
 
 
 def on_device(tokens, norm_gain, in_weight, filter_taps, conv_skip, out_weight):
-    whole = lax.all_gather(tokens, ("trow", "tcol"), axis=1, tiled=True)
+    whole = collect(tokens, ("trow", "tcol"), 1)
     wide = whole.astype(jnp.float32)
     mean_square = jnp.mean(wide * wide, axis=1, keepdims=True)
     normed = (wide * lax.rsqrt(mean_square + 1e-06) * norm_gain).astype(jnp.bfloat16)

time: 222 us -> 261 us (1.18)
  starting transfers between devices: 3.13 us -> 63.4 us
  waiting for transfers between devices: 140 us -> 100 us
  local copies, waits for them, and re-layouts: 16.9 us -> 31.2 us
    ppermute x0 -> x15, starting transfers between devices: none -> 60.1 us  [the longest x7 41.8 us: collect(): from_right = lax.ppermute(from_right, axis, backward)]
    all_gather x1 -> x0, waiting for transfers between devices: 59.9 us -> none  [on_device(): whole = lax.all_gather(tokens, ('trow', 'tcol'), axis=1, tiled=True)]
    ppermute x0 -> x15, waiting for transfers between devices: none -> 23.2 us  [the longest x8 15.7 us: collect(): from_left = lax.ppermute(from_left, axis, upward)]
    dynamic_update_slice x0 -> x16, local copies, waits for them, and re-layouts: none -> 12 us  [the longest x8 6.01 us: collect(): lax.dynamic_update_slice_in_dim(out, from_left, (index - hop) % count * w...]
    reduce_scatter x1, waiting for transfers between devices: 77 us -> 74.3 us  [on_device(): lax.psum_scatter(partial_sum.astype(jnp.bfloat16), ('trow', 'tcol'), scat...]
  transfers between devices with their start and end apart: 3 -> 17, of which waited for: 3 -> 12; matrix products, arithmetic and copies ran while one was open for 0% -> 5% of each run, Pallas kernels for 0% -> 0%
where the time goes in v1:
time: 261 us; the launch traced here: 259 us
  waiting for transfers between devices  100 us (38%)
  starting transfers between devices  63.4 us (24%)
  local copies, waits for them, and re-layouts  31.2 us (12%)
  other arithmetic  25.2 us (10%)
  matrix products  22.9 us (9%)
  between operations  13.6 us (5%)
    reduce_scatter x1, waiting for transfers between devices, on_device(): lax.psum_scatter(partial_sum.astype(jnp.bfloat16), ('trow', 'tcol'), scat...  74.3 us
    ppermute x7, starting transfers between devices, collect(): from_right = lax.ppermute(from_right, axis, backward)  41.8 us
    add x16, other arithmetic, tap_group(): total = total + window.astype(jnp.float32) * weight  21.9 us
    ppermute x8, starting transfers between devices, collect(): from_left = lax.ppermute(from_left, axis, upward)  18.3 us
    dynamic_slice x16, local copies, waits for them, and re-layouts, tap_group(): weight = lax.dynamic_slice_in_dim(filter_taps, index, 1, 0)  16.6 us
    ppermute x8, waiting for transfers between devices, collect(): from_left = lax.ppermute(from_left, axis, upward)  15.7 us
    dot_general x1, matrix products, on_device(): partial_sum = jnp.dot(gated, out_weight, preferred_element_type=jnp.float32)  11.2 us
    ppermute x7, waiting for transfers between devices, collect(): from_right = lax.ppermute(from_right, axis, backward)  7.56 us
  transfers between devices with their start and end apart: 17, of which 12 were waited for; matrix products, arithmetic and copies ran while one was open for 5% of the time, Pallas kernels for 0%

profile of v1, /device:TPU:1, one launch (start us, length us, event | category | flops | bytes accessed | tf_op | source)
XLA Modules:
  0.0 258.6 jit_solution(4573460136492094979)
XLA Ops:
  6.5 4.9 %collective-permute-start = (bf16[512,256]{1,0:T(8,128)(2,1)}, bf16[512,256]{1,0:T(8,128)(2,1)S(1)}, u32[]{:S(2)}, u32[]{:S(2)}) collective-permute-start(bf16[512,256]{1,0:T(8,128)(2,1)} %param.8), channel_id=1, source_target_pairs={{0,1},{1,2},{2,3},{3,4},{4,5},{5,6},{6,7},{7,8},{8,9},{9,10},{10,1... | collective-permute-start | bytes 786440 | tf_op jit(solution)/shard_map/ppermute | solution.py:16
  11.5 9.1 %collective-permute-start.1 = (bf16[512,256]{1,0:T(8,128)(2,1)}, bf16[512,256]{1,0:T(8,128)(2,1)S(1)}, u32[]{:S(2)}, u32[]{:S(2)}) collective-permute-start(bf16[512,256]{1,0:T(8,128)(2,1)} %param.8), channel_id=1, source_target_pairs={{0,15},{1,0},{2,1},{3,2},{4,3},{5,4},{6,5},{7,6},{8,7},{9,8},{10,9... | collective-permute-start | bytes 786440 | tf_op jit(solution)/shard_map/ppermute | solution.py:21
  20.7 4.3 %collective-permute-done = bf16[512,256]{1,0:T(8,128)(2,1)S(1)} collective-permute-done((bf16[512,256]{1,0:T(8,128)(2,1)}, bf16[512,256]{1,0:T(8,128)(2,1)S(1)}, u32[]{:S(2)}, u32[]{:S(2)}) %collective-permute-start) | collective-permute-done | bytes 262176 | tf_op jit(solution)/shard_map/ppermute | solution.py:16
  24.9 1.9 collective-permute-start.2
  27.1 5.5 %collective-permute-start.3 = (bf16[512,256]{1,0:T(8,128)(2,1)S(1)}, bf16[512,256]{1,0:T(8,128)(2,1)S(1)}, u32[]{:S(2)}, u32[]{:S(2)}) collective-permute-start(bf16[512,256]{1,0:T(8,128)(2,1)S(1)} %collective-permute-done.1), channel_id=1, source_target_pairs={{0,15},{1,0},{2,1},{3,2},{4,3},{5,4},{6,5},{7,6},{8,7},{9,8},{10,9... | collective-permute-start | bytes 786440 | tf_op jit(solution)/shard_map/ppermute | solution.py:21
  32.5 3.2 %collective-permute-done.2 = bf16[512,256]{1,0:T(8,128)(2,1)S(1)} collective-permute-done((bf16[512,256]{1,0:T(8,128)(2,1)S(1)}, bf16[512,256]{1,0:T(8,128)(2,1)S(1)}, u32[]{:S(2)}, u32[]{:S(2)}) %collective-permute-start.2) | collective-permute-done | bytes 262176 | tf_op jit(solution)/shard_map/ppermute | solution.py:16
  35.8 1.9 collective-permute-start.4
  38.4 5.6 %collective-permute-start.5 = (bf16[512,256]{1,0:T(8,128)(2,1)S(1)}, bf16[512,256]{1,0:T(8,128)(2,1)S(1)}, u32[]{:S(2)}, u32[]{:S(2)}) collective-permute-start(bf16[512,256]{1,0:T(8,128)(2,1)S(1)} %collective-permute-done.3), channel_id=1, source_target_pairs={{0,15},{1,0},{2,1},{3,2},{4,3},{5,4},{6,5},{7,6},{8,7},{9,8},{10,9... | collective-permute-start | bytes 786440 | tf_op jit(solution)/shard_map/ppermute | solution.py:21
  44.0 2.7 %collective-permute-done.4 = bf16[512,256]{1,0:T(8,128)(2,1)S(1)} collective-permute-done((bf16[512,256]{1,0:T(8,128)(2,1)S(1)}, bf16[512,256]{1,0:T(8,128)(2,1)S(1)}, u32[]{:S(2)}, u32[]{:S(2)}) %collective-permute-start.4) | collective-permute-done | bytes 262176 | tf_op jit(solution)/shard_map/ppermute | solution.py:16
  46.7 1.9 collective-permute-start.6
  48.6 2.5 broadcast_in_dim.4
  52.6 4.8 %collective-permute-start.7 = (bf16[512,256]{1,0:T(8,128)(2,1)S(1)}, bf16[512,256]{1,0:T(8,128)(2,1)S(1)}, u32[]{:S(2)}, u32[]{:S(2)}) collective-permute-start(bf16[512,256]{1,0:T(8,128)(2,1)S(1)} %collective-permute-done.5), channel_id=1, source_target_pairs={{0,15},{1,0},{2,1},{3,2},{4,3},{5,4},{6,5},{7,6},{8,7},{9,8},{10,9... | collective-permute-start | bytes 786440 | tf_op jit(solution)/shard_map/ppermute | solution.py:21
  58.2 1.9 collective-permute-start.8
  61.7 1.8 collective-permute-done.7
  63.5 5.6 %collective-permute-start.9 = (bf16[512,256]{1,0:T(8,128)(2,1)S(1)}, bf16[512,256]{1,0:T(8,128)(2,1)S(1)}, u32[]{:S(2)}, u32[]{:S(2)}) collective-permute-start(bf16[512,256]{1,0:T(8,128)(2,1)S(1)} %collective-permute-done.7), channel_id=1, source_target_pairs={{0,15},{1,0},{2,1},{3,2},{4,3},{5,4},{6,5},{7,6},{8,7},{9,8},{10,9... | collective-permute-start | bytes 786440 | tf_op jit(solution)/shard_map/ppermute | solution.py:21
  69.8 1.9 collective-permute-start.10
  73.3 1.6 collective-permute-done.9
  74.9 5.6 %collective-permute-start.11 = (bf16[512,256]{1,0:T(8,128)(2,1)S(1)}, bf16[512,256]{1,0:T(8,128)(2,1)S(1)}, u32[]{:S(2)}, u32[]{:S(2)}) collective-permute-start(bf16[512,256]{1,0:T(8,128)(2,1)S(1)} %collective-permute-done.9), channel_id=1, source_target_pairs={{0,15},{1,0},{2,1},{3,2},{4,3},{5,4},{6,5},{7,6},{8,7},{9,8},{10,9... | collective-permute-start | bytes 786440 | tf_op jit(solution)/shard_map/ppermute | solution.py:21
  81.3 1.9 collective-permute-start.12
  84.7 1.6 collective-permute-done.11
  86.3 5.6 %collective-permute-start.13 = (bf16[512,256]{1,0:T(8,128)(2,1)S(1)}, bf16[512,256]{1,0:T(8,128)(2,1)S(1)}, u32[]{:S(2)}, u32[]{:S(2)}) collective-permute-start(bf16[512,256]{1,0:T(8,128)(2,1)S(1)} %collective-permute-done.11), channel_id=1, source_target_pairs={{0,15},{1,0},{2,1},{3,2},{4,3},{5,4},{6,5},{7,6},{8,7},{9,8},{10,9... | collective-permute-start | bytes 786440 | tf_op jit(solution)/shard_map/ppermute | solution.py:21
  92.6 1.9 collective-permute-start.14
  96.0 1.7 collective-permute-done.13
  98.4 5.4 %collective-permute-done.14 = bf16[512,256]{1,0:T(8,128)(2,1)S(1)} collective-permute-done((bf16[512,256]{1,0:T(8,128)(2,1)S(1)}, bf16[512,256]{1,0:T(8,128)(2,1)S(1)}, u32[]{:S(2)}, u32[]{:S(2)}) %collective-permute-start.14) | collective-permute-done | bytes 262176 | tf_op jit(solution)/shard_map/ppermute | solution.py:16
  104.6 3.1 %fusion.7 = f32[512]{0:T(512)S(1)} fusion(bf16[512,4096]{1,0:T(8,128)(2,1)} %constant_dynamic-update-slice_fusion), kind=kLoop, calls=%fused_computation.18 | loop fusion | flops 6290944 | bytes 4196352 | tf_op jit(solution)/shard_map/reduce_sum | solution.py:37
  107.7 5.8 %fusion.46 = f32[512,512]{1,0:T(8,128)S(1)} fusion(bf16[3,4096,512]{2,1,0:T(8,128)(2,1)} %param.10, bf16[512,4096]{1,0:T(8,128)(2,1)} %constant_dynamic-update-slice_fusion, f32[4096]{0:T(1024)S(1)} %copy-done.1, f32[512]{0:T(512)S(1)} %add_rsqrt_fusion), kind=kOutput, calls=%fused_computation.40 | convolution fusion | flops 2156396544 | bytes 9455616 | tf_op jit(solution)/shard_map/dot_general | solution.py:41
  113.5 5.8 %fusion.40 = bf16[512,512]{1,0:T(8,128)(2,1)S(1)} fusion(f32[512,512]{1,0:T(8,128)S(1)} %fusion.46, bf16[3,4096,512]{2,1,0:T(8,128)(2,1)} %param.10, bf16[512,4096]{1,0:T(8,128)(2,1)} %constant_dynamic-update-slice_fusion, f32[4096]{0:T(1024)S(1)} %copy-done.1, f32[512]{0:T(512)S(1)} %add_rsqrt_fusion), kind=kOutput, calls=%fused_computation.38 | convolution fusion | flops 2156920832 | bytes 9979904 | tf_op jit(solution)/shard_map/dot_general | solution.py:40
  119.4 3.3 %collective-permute-start.15 = (bf16[127,512]{1,0:T(8,128)(2,1)S(1)}, bf16[127,512]{1,0:T(8,128)(2,1)S(1)}, u32[]{:S(2)}, u32[]{:S(2)}) collective-permute-start(bf16[127,512]{1,0:T(8,128)(2,1)S(1)} %slice.16), channel_id=1, source_target_pairs={{0,16},{16,32},{32,48},{48,64},{64,80},{80,96},{96,112},{112,128},... | collective-permute-start | bytes 390152 | tf_op jit(solution)/shard_map/ppermute | solution.py:31
  122.7 2.4 collective-permute-done.15
  125.3 40.9 %while.17 = (s32[]{:T(128)}, f32[512,512]{1,0:T(8,128)S(1)}, bf16[639,512]{1,0:T(8,128)(2,1)S(1)}, f32[128,512]{1,0:T(8,128)}, s32[]{:T(128)}, /*index=5*/s32[]{...) while((s32[]{:T(128)}, f32[512,512]{1,0:T(8,128)S(1)}, ...), condition=%wide.region_2.3_spmd.clone, body=%wide.region_1.2_spmd.clone.sunk | while | flops 6553667 | bytes 6341623 | solution.py:58
  166.2 11.2 %convolution_convert_fusion = bf16[512,4096]{1,0:T(8,128)(2,1)} fusion(bf16[512,4096]{1,0:T(8,128)(2,1)} %param.13, bf16[3,4096,512]{2,1,0:T(8,128)(2,1)} %param.10, f32[512,512]{1,0:T(8,128)S(1)} %get-tuple-element.156, bf16[512,512]{1,0:T(8,128)(2,1)S(1)} %fusion.40, f32[512]{0:T(512)S(1)} %copy-done.2, ...), kind=kOutput, calls=%fused_computation.21 | convolution fusion | flops 4307288064 | bytes 18370560 | tf_op jit(solution)/shard_map/dot_general | solution.py:61
  177.5 74.3 %reduce-scatter.2.cloned.1.call-done = bf16[512,256]{1,0:T(8,128)(2,1)} async-done(((bf16[512,4096]{1,0:T(8,128)(2,1)}), bf16[512,256]{1,0:T(8,128)(2,1)}) %reduce-scatter.2.cloned.1.call-update) | async-done | bytes 262160 | tf_op jit(solution)/shard_map/reduce_scatter | solution.py:62
  (67 shorter events, 51.7 us)
Async XLA Ops:
  6.5 44.5 %copy-start = (bf16[512,256]{1,0:T(8,128)(2,1)S(1)}, bf16[512,256]{1,0:T(8,128)(2,1)}, u32[]{:S(2)}) copy-start(bf16[512,256]{1,0:T(8,128)(2,1)} %param.8) | copy-start | bytes 786436
  6.5 245.2 %reduce-scatter.2.cloned.1.call-start = ((), (), s32[]{:S(2)}) async-start(), calls=%async_computation.1 | async-start | bytes 4456448 | tf_op jit(solution)/shard_map/reduce_scatter | solution.py:62
  6.5 18.4 %collective-permute-start = (bf16[512,256]{1,0:T(8,128)(2,1)}, bf16[512,256]{1,0:T(8,128)(2,1)S(1)}, u32[]{:S(2)}, u32[]{:S(2)}) collective-permute-start(bf16[512,256]{1,0:T(8,128)(2,1)} %param.8), channel_id=1, source_target_pairs={{0,1},{1,2},{2,3},{3,4},{4,5},{5,6},{6,7},{7,8},{8,9},{9,10},{10,1... | collective-permute-start | bytes 786440 | tf_op jit(solution)/shard_map/ppermute | solution.py:16
  11.5 15.6 %collective-permute-start.1 = (bf16[512,256]{1,0:T(8,128)(2,1)}, bf16[512,256]{1,0:T(8,128)(2,1)S(1)}, u32[]{:S(2)}, u32[]{:S(2)}) collective-permute-start(bf16[512,256]{1,0:T(8,128)(2,1)} %param.8), channel_id=1, source_target_pairs={{0,15},{1,0},{2,1},{3,2},{4,3},{5,4},{6,5},{7,6},{8,7},{9,8},{10,9... | collective-permute-start | bytes 786440 | tf_op jit(solution)/shard_map/ppermute | solution.py:21
  24.9 10.9 %collective-permute-start.2 = (bf16[512,256]{1,0:T(8,128)(2,1)S(1)}, bf16[512,256]{1,0:T(8,128)(2,1)S(1)}, u32[]{:S(2)}, u32[]{:S(2)}) collective-permute-start(bf16[512,256]{1,0:T(8,128)(2,1)S(1)} %collective-permute-done), channel_id=1, source_target_pairs={{0,1},{1,2},{2,3},{3,4},{4,5},{5,6},{6,7},{7,8},{8,9},{9,10},{10,1... | collective-permute-start | bytes 786440 | tf_op jit(solution)/shard_map/ppermute | solution.py:16
  27.1 11.3 %collective-permute-start.3 = (bf16[512,256]{1,0:T(8,128)(2,1)S(1)}, bf16[512,256]{1,0:T(8,128)(2,1)S(1)}, u32[]{:S(2)}, u32[]{:S(2)}) collective-permute-start(bf16[512,256]{1,0:T(8,128)(2,1)S(1)} %collective-permute-done.1), channel_id=1, source_target_pairs={{0,15},{1,0},{2,1},{3,2},{4,3},{5,4},{6,5},{7,6},{8,7},{9,8},{10,9... | collective-permute-start | bytes 786440 | tf_op jit(solution)/shard_map/ppermute | solution.py:21
  35.8 10.9 %collective-permute-start.4 = (bf16[512,256]{1,0:T(8,128)(2,1)S(1)}, bf16[512,256]{1,0:T(8,128)(2,1)S(1)}, u32[]{:S(2)}, u32[]{:S(2)}) collective-permute-start(bf16[512,256]{1,0:T(8,128)(2,1)S(1)} %collective-permute-done.2), channel_id=1, source_target_pairs={{0,1},{1,2},{2,3},{3,4},{4,5},{5,6},{6,7},{7,8},{8,9},{9,10},{10,1... | collective-permute-start | bytes 786440 | tf_op jit(solution)/shard_map/ppermute | solution.py:16
  38.4 14.2 %collective-permute-start.5 = (bf16[512,256]{1,0:T(8,128)(2,1)S(1)}, bf16[512,256]{1,0:T(8,128)(2,1)S(1)}, u32[]{:S(2)}, u32[]{:S(2)}) collective-permute-start(bf16[512,256]{1,0:T(8,128)(2,1)S(1)} %collective-permute-done.3), channel_id=1, source_target_pairs={{0,15},{1,0},{2,1},{3,2},{4,3},{5,4},{6,5},{7,6},{8,7},{9,8},{10,9... | collective-permute-start | bytes 786440 | tf_op jit(solution)/shard_map/ppermute | solution.py:21
  46.7 11.5 %collective-permute-start.6 = (bf16[512,256]{1,0:T(8,128)(2,1)S(1)}, bf16[512,256]{1,0:T(8,128)(2,1)S(1)}, u32[]{:S(2)}, u32[]{:S(2)}) collective-permute-start(bf16[512,256]{1,0:T(8,128)(2,1)S(1)} %collective-permute-done.4), channel_id=1, source_target_pairs={{0,1},{1,2},{2,3},{3,4},{4,5},{5,6},{6,7},{7,8},{8,9},{9,10},{10,1... | collective-permute-start | bytes 786440 | tf_op jit(solution)/shard_map/ppermute | solution.py:16
  52.6 10.9 %collective-permute-start.7 = (bf16[512,256]{1,0:T(8,128)(2,1)S(1)}, bf16[512,256]{1,0:T(8,128)(2,1)S(1)}, u32[]{:S(2)}, u32[]{:S(2)}) collective-permute-start(bf16[512,256]{1,0:T(8,128)(2,1)S(1)} %collective-permute-done.5), channel_id=1, source_target_pairs={{0,15},{1,0},{2,1},{3,2},{4,3},{5,4},{6,5},{7,6},{8,7},{9,8},{10,9... | collective-permute-start | bytes 786440 | tf_op jit(solution)/shard_map/ppermute | solution.py:21
  58.2 11.6 %collective-permute-start.8 = (bf16[512,256]{1,0:T(8,128)(2,1)S(1)}, bf16[512,256]{1,0:T(8,128)(2,1)S(1)}, u32[]{:S(2)}, u32[]{:S(2)}) collective-permute-start(bf16[512,256]{1,0:T(8,128)(2,1)S(1)} %collective-permute-done.6), channel_id=1, source_target_pairs={{0,1},{1,2},{2,3},{3,4},{4,5},{5,6},{6,7},{7,8},{8,9},{9,10},{10,1... | collective-permute-start | bytes 786440 | tf_op jit(solution)/shard_map/ppermute | solution.py:16
  63.5 11.4 %collective-permute-start.9 = (bf16[512,256]{1,0:T(8,128)(2,1)S(1)}, bf16[512,256]{1,0:T(8,128)(2,1)S(1)}, u32[]{:S(2)}, u32[]{:S(2)}) collective-permute-start(bf16[512,256]{1,0:T(8,128)(2,1)S(1)} %collective-permute-done.7), channel_id=1, source_target_pairs={{0,15},{1,0},{2,1},{3,2},{4,3},{5,4},{6,5},{7,6},{8,7},{9,8},{10,9... | collective-permute-start | bytes 786440 | tf_op jit(solution)/shard_map/ppermute | solution.py:21
  69.8 11.4 %collective-permute-start.10 = (bf16[512,256]{1,0:T(8,128)(2,1)S(1)}, bf16[512,256]{1,0:T(8,128)(2,1)S(1)}, u32[]{:S(2)}, u32[]{:S(2)}) collective-permute-start(bf16[512,256]{1,0:T(8,128)(2,1)S(1)} %collective-permute-done.8), channel_id=1, source_target_pairs={{0,1},{1,2},{2,3},{3,4},{4,5},{5,6},{6,7},{7,8},{8,9},{9,10},{10,1... | collective-permute-start | bytes 786440 | tf_op jit(solution)/shard_map/ppermute | solution.py:16
  73.3 34.4 %copy-start.1 = (f32[4096]{0:T(1024)S(1)}, f32[4096]{0:T(1024)}, u32[]{:S(2)}) copy-start(f32[4096]{0:T(1024)} %param.9) | copy-start | bytes 49156
  74.9 11.4 %collective-permute-start.11 = (bf16[512,256]{1,0:T(8,128)(2,1)S(1)}, bf16[512,256]{1,0:T(8,128)(2,1)S(1)}, u32[]{:S(2)}, u32[]{:S(2)}) collective-permute-start(bf16[512,256]{1,0:T(8,128)(2,1)S(1)} %collective-permute-done.9), channel_id=1, source_target_pairs={{0,15},{1,0},{2,1},{3,2},{4,3},{5,4},{6,5},{7,6},{8,7},{9,8},{10,9... | collective-permute-start | bytes 786440 | tf_op jit(solution)/shard_map/ppermute | solution.py:21
  81.3 11.4 %collective-permute-start.12 = (bf16[512,256]{1,0:T(8,128)(2,1)S(1)}, bf16[512,256]{1,0:T(8,128)(2,1)S(1)}, u32[]{:S(2)}, u32[]{:S(2)}) collective-permute-start(bf16[512,256]{1,0:T(8,128)(2,1)S(1)} %collective-permute-done.10), channel_id=1, source_target_pairs={{0,1},{1,2},{2,3},{3,4},{4,5},{5,6},{6,7},{7,8},{8,9},{9,10},{10,1... | collective-permute-start | bytes 786440 | tf_op jit(solution)/shard_map/ppermute | solution.py:16
  86.3 11.4 %collective-permute-start.13 = (bf16[512,256]{1,0:T(8,128)(2,1)S(1)}, bf16[512,256]{1,0:T(8,128)(2,1)S(1)}, u32[]{:S(2)}, u32[]{:S(2)}) collective-permute-start(bf16[512,256]{1,0:T(8,128)(2,1)S(1)} %collective-permute-done.11), channel_id=1, source_target_pairs={{0,15},{1,0},{2,1},{3,2},{4,3},{5,4},{6,5},{7,6},{8,7},{9,8},{10,9... | collective-permute-start | bytes 786440 | tf_op jit(solution)/shard_map/ppermute | solution.py:21
  92.6 11.2 %collective-permute-start.14 = (bf16[512,256]{1,0:T(8,128)(2,1)S(1)}, bf16[512,256]{1,0:T(8,128)(2,1)S(1)}, u32[]{:S(2)}, u32[]{:S(2)}) collective-permute-start(bf16[512,256]{1,0:T(8,128)(2,1)S(1)} %collective-permute-done.12), channel_id=1, source_target_pairs={{0,1},{1,2},{2,3},{3,4},{4,5},{5,6},{6,7},{7,8},{8,9},{9,10},{10,1... | collective-permute-start | bytes 786440 | tf_op jit(solution)/shard_map/ppermute | solution.py:16
  119.4 5.7 %collective-permute-start.15 = (bf16[127,512]{1,0:T(8,128)(2,1)S(1)}, bf16[127,512]{1,0:T(8,128)(2,1)S(1)}, u32[]{:S(2)}, u32[]{:S(2)}) collective-permute-start(bf16[127,512]{1,0:T(8,128)(2,1)S(1)} %slice.16), channel_id=1, source_target_pairs={{0,16},{16,32},{32,48},{48,64},{64,80},{80,96},{96,112},{112,128},... | collective-permute-start | bytes 390152 | tf_op jit(solution)/shard_map/ppermute | solution.py:31
  125.3 40.9 %copy-start.2 = (f32[512]{0:T(512)S(1)}, f32[512]{0:T(512)}, u32[]{:S(2)}) copy-start(f32[512]{0:T(512)} %param.12) | copy-start | bytes 6148
Sparse Core Ops, SparseCore 0:
  177.6 74.1 reduce-scatter.1
